TPU v7x, 128 devices: a whole 4x4x4 slice. The times are simulated.
128 devices in a mesh: seq: 32 (over z, y, core), head: 4 (over x).
Axes of the slice: x: 4, y: 4, z: 4, core: 2. Of those that a mesh axis runs over, the one named last changes fastest.
Arguments:
- tokens: bfloat16 [65536, 1024], P(('seq', 'head')), may hold values from -6 to 6
- w_gate_x: bfloat16 [1024, 4096], replicated, may hold values from -0.1875 to 0.1875
- w_bc_dt: bfloat16 [1024, 160], replicated, may hold values from -0.1875 to 0.1875
- conv_x_weight: float32 [4, 2048], P(None, 'head'), may hold values from -0.5 to 0.5
- conv_x_bias: float32 [2048], P('head'), may hold values from -0.5 to 0.5
- conv_bc_weight: float32 [4, 128], replicated, may hold values from -0.5 to 0.5
- conv_bc_bias: float32 [128], replicated, may hold values from -0.5 to 0.5
- dt_bias: float32 [32], P('head'), may hold values from -9 to -1
- a_log: float32 [32], P('head'), may hold values from -4 to 1
- skip_d: float32 [32], P('head'), may hold values from 0.5 to 1.5
- norm_gain: float32 [2048], replicated, may hold values from 0.1 to 1.9
- w_out: bfloat16 [2048, 1024], replicated, may hold values from -0.125 to 0.125
Outputs:
- mixed: bfloat16 [65536, 1024], P(('seq', 'head'))
All inputs are finite; a program needn't handle non-finite values.
Results may differ from a plain program's by a relative error of at most 0.009.
Values may be sent and summed in bfloat16 or wider, within the bound.
No kernel may reach another device: no remote copies, remote signals or barrier semaphores. Data moves between devices by JAX's collectives and lax.ppermute only.
A program may use at most 128 MiB of HBM per device.

v0:
```python
import jax
import jax.numpy as jnp
from jax import lax
from jax.sharding import PartitionSpec as P

HEADS = 32
HEAD_DIM = 64
STATE = 64
GROUP = 256
CONV = 4
epsilon = 1e-05


def from_behind(array, axis, by):
    size = lax.axis_size(axis)
    pairs = [(i, i + by) for i in range(size) if 0 <= i + by < size]
    return lax.ppermute(array, axis, pairs)


def prefix(array, axis, combine, identity):
    size, mine = (lax.axis_size(axis), lax.axis_index(axis))
    everything = jax.tree.map(lambda part: lax.all_gather(part, axis), array)
    start = jax.tree.map(
        lambda part, zero: jnp.broadcast_to(jnp.asarray(zero, part.dtype), part.shape),
        array,
        identity,
    )

    def hop(k, before):
        reached = k < mine
        new = combine(before, jax.tree.map(lambda part: part[k], everything))
        return jax.tree.map(lambda a, b: jnp.where(reached, a, b), new, before)

    return lax.fori_loop(0, size, hop, start)


def causal_taps(padded, weights, biases, count):
    summed = biases + weights[0] * padded[0:count]
    for tap_index in range(1, CONV):
        summed = summed + weights[tap_index] * padded[tap_index : tap_index + count]
    return jax.nn.silu(summed).astype(jnp.bfloat16)


def on_device(
    tokens,
    w_gate_x,
    w_bc_dt,
    conv_x_weight,
    conv_x_bias,
    conv_bc_weight,
    conv_bc_bias,
    dt_bias,
    a_log,
    skip_d,
    norm_gain,
    w_out,
):
    highest = lax.Precision.HIGHEST
    heads_here = dt_bias.shape[0]
    dinner_here = heads_here * HEAD_DIM
    tok_rows = tokens.shape[0]
    gate_all = jnp.dot(tokens, w_gate_x, preferred_element_type=jnp.float32).astype(jnp.bfloat16)
    gate_all = gate_all.reshape(tok_rows, HEADS, 2 * HEAD_DIM)
    bc_dt = jnp.dot(tokens, w_bc_dt, preferred_element_type=jnp.float32).astype(jnp.bfloat16)
    dt_all = bc_dt[:, 2 * STATE :].reshape(tok_rows, HEADS, 1)
    gate_x, dt_raw = (
        lax.all_to_all(gate_all, "head", split_axis=1, concat_axis=0, tiled=True),
        lax.all_to_all(dt_all, "head", split_axis=1, concat_axis=0, tiled=True),
    )
    dt_raw = dt_raw[:, :, 0]
    bc_rows = lax.all_gather(bc_dt[:, : 2 * STATE], "head", axis=0, tiled=True)
    seq_rows = gate_x.shape[0]
    gate_z = gate_x[:, :, :HEAD_DIM]
    x_chan = gate_x[:, :, HEAD_DIM:].reshape(seq_rows, dinner_here)
    conv_input = jnp.concatenate([x_chan, bc_rows], axis=1)
    rim_rows = from_behind(conv_input[seq_rows - (CONV - 1) :], "seq", 1)
    padded = jnp.concatenate([rim_rows, conv_input], axis=0).astype(jnp.float32)
    conv_weights = jnp.concatenate([conv_x_weight, conv_bc_weight], axis=1)
    conv_biases = jnp.concatenate([conv_x_bias, conv_bc_bias], axis=0)
    conved = causal_taps(padded, conv_weights, conv_biases, seq_rows)
    x_heads = conved[:, :dinner_here].astype(jnp.float32).reshape(seq_rows, heads_here, HEAD_DIM)
    b_mat = conved[:, dinner_here : dinner_here + STATE].astype(jnp.float32)
    c_mat = conved[:, dinner_here + STATE :].astype(jnp.float32)
    dt_step = jax.nn.softplus(dt_raw.astype(jnp.float32) + dt_bias)
    log_decay = dt_step * -jnp.exp(a_log)
    x_dt = x_heads * dt_step[:, :, None]
    blocks = seq_rows // GROUP
    decay_blocks = log_decay.reshape(blocks, GROUP, heads_here)
    xdt_blocks = x_dt.reshape(blocks, GROUP, heads_here, HEAD_DIM)
    b_blocks = b_mat.reshape(blocks, GROUP, STATE)
    c_blocks = c_mat.reshape(blocks, GROUP, STATE)
    cumlog = jnp.cumsum(decay_blocks, axis=1)
    scores = jnp.einsum("ktn,ksn->kts", c_blocks, b_blocks, precision=highest)
    by_head = jnp.swapaxes(cumlog, 1, 2)
    gaps = by_head[:, :, :, None] - by_head[:, :, None, :]
    causal = jnp.arange(GROUP)[:, None] >= jnp.arange(GROUP)[None, :]
    decays = jnp.where(causal[None, None], jnp.exp(jnp.minimum(gaps, 0.0)), 0.0)
    mixed = scores[:, None] * decays
    y_intra = jnp.einsum("khts,kshp->kthp", mixed, xdt_blocks, precision=highest)
    block_ends = cumlog[:, -1, :]
    to_end = jnp.exp(block_ends[:, None, :] - cumlog)
    local_states = jnp.einsum(
        "kshp,ksn->khpn", to_end[..., None] * xdt_blocks, b_blocks, precision=highest
    )

    def chain_step(carried, inputs):
        block_decay, fresh = inputs
        return (block_decay[:, None, None] * carried + fresh, carried)

    zero_state = jnp.zeros((heads_here, HEAD_DIM, STATE), jnp.float32)
    device_state, block_starts = lax.scan(
        chain_step, zero_state, (jnp.exp(block_ends), local_states)
    )
    total_log = jnp.sum(block_ends, axis=0)

    def combine(earlier, latter):
        return (earlier[0] + latter[0], earlier[1] * jnp.exp(latter[0])[:, None, None] + latter[1])

    prefix_log, incoming = prefix(
        (total_log, device_state), "seq", combine, (jnp.zeros_like(total_log), zero_state)
    )
    offset = jnp.cumsum(block_ends, axis=0) - block_ends
    start_states = block_starts + jnp.exp(offset)[:, :, None, None] * incoming[None]
    y_state = jnp.exp(cumlog)[..., None] * jnp.einsum(
        "ktn,khpn->kthp", c_blocks, start_states, precision=highest
    )
    y_heads = (y_intra + y_state).reshape(seq_rows, heads_here, HEAD_DIM) + skip_d[
        None, :, None
    ] * x_heads
    gated_out = (
        (y_heads * jax.nn.silu(gate_z.astype(jnp.float32)))
        .astype(jnp.bfloat16)
        .reshape(seq_rows, dinner_here)
    )
    by_token = lax.all_to_all(gated_out, "head", split_axis=0, concat_axis=1, tiled=True)
    gated_f = by_token.astype(jnp.float32)
    mean_sq = jnp.mean(gated_f * gated_f, axis=1, keepdims=True)
    normed = (gated_f * lax.rsqrt(mean_sq + epsilon) * norm_gain).astype(jnp.bfloat16)
    return jnp.dot(normed, w_out, preferred_element_type=jnp.float32).astype(jnp.bfloat16)


def solution(mesh):
    return jax.shard_map(
        on_device,
        mesh=mesh,
        in_specs=(
            P(("seq", "head"), None),
            P(),
            P(),
            P(None, "head"),
            P("head"),
            P(),
            P(),
            P("head"),
            P("head"),
            P("head"),
            P(),
            P(),
        ),
        out_specs=P(("seq", "head"), None),
        check_vma=False,
    )
```

profile of v0, /device:TPU:0, one launch (start us, length us, event | category | flops | bytes accessed | tf_op | source)
XLA Modules:
  0.0 321.6 jit_solution(6159652783522887039)
XLA Ops:
  6.5 1.2 copy-done
  7.8 1.5 convolution_convert_fusion.2
  9.8 0.8 reduce.13
  11.3 4.4 %all-to-all-start.1 = ((bf16[4,2,2048]{2,1,0:T(2,128)(2,1)}), bf16[4,2,2048]{2,1,0:T(2,128)(2,1)S(1)}, u32[]{:S(2)}, u32[]{:S(2)}) async-start(bf16[4,2,2048]{2,1,0:T(2,128)(2,1)} %reshape.184), calls=%async_computation.1 | async-start | bytes 65536 | tf_op jit(solution)/shard_map/all_to_all | solution.py:68
  15.7 8.1 %fusion.28 = bf16[64,32,8,128]{3,2,1,0:T(8,128)(2,1)S(1)} fusion(bf16[512,1024]{1,0:T(8,128)(2,1)S(1)} %copy-done, bf16[1024,4096]{1,0:T(8,128)(2,1)} %param.17), kind=kOutput, calls=%fused_computation.46 | convolution fusion | flops 4297064448 | bytes 13631488 | tf_op jit(solution)/shard_map/dot_general | solution.py:62
  23.8 3.1 copy.123
  27.0 5.0 %all-to-all-start = ((bf16[512,32,128]{2,0,1:T(8,128)(2,1)}), bf16[512,32,128]{2,0,1:T(8,128)(2,1)}, u32[]{:S(2)}, u32[]{:S(2)}) async-start(bf16[512,32,128]{2,0,1:T(8,128)(2,1)} %bitcast.113), calls=%async_computation | async-start | bytes 8388608 | tf_op jit(solution)/shard_map/all_to_all | solution.py:67
  32.2 56.7 %all_gather.15 = bf16[2048,128]{0,1:T(8,128)(2,1)S(1)} all-gather(bf16[512,128]{0,1:T(8,128)(2,1)S(1)} %slice.78), channel_id=1, replica_groups=mesh['seq'=32,'head'=4] {'head'}, dimensions={0}, use_global_device_ids=true | all-gather | bytes 655360 | tf_op jit(solution)/shard_map/all_gather | solution.py:71
  89.1 4.5 %reduce-window.6 = f32[8,8,2,128]{3,1,2,0:T(8,128)S(1)} reduce-window(f32[8,8,2,128]{3,1,2,0:T(8,128)S(1)} %get-tuple-element.196, f32[]{:T(128)} %constant.58.clone.1), window={size=1x1x1x128 pad=0_0x0_0x0_0x127_0}, to_apply=%region_0.1 | reduce-window | flops 2080768 | bytes 131076 | tf_op jit(solution)/shard_map/reduce-window
  94.4 4.9 %copy.73 = bf16[4,512,8,128]{3,2,1,0:T(8,128)(2,1)S(1)} copy(bf16[4,512,8,128]{3,1,2,0:T(8,128)(2,1)} %bitcast.2) | data formatting | bytes 8388608 | tf_op jit(solution)/shard_map/all_to_all | solution.py:67
  99.3 4.0 %fusion.44 = (bf16[2048,8,64]{2,1,0:T(8,128)(2,1)}, bf16[2048,8,64]{2,1,0:T(8,128)(2,1)}) fusion(bf16[2048,8,128]{2,1,0:T(8,128)(2,1)S(1)} %bitcast.109), kind=kLoop, calls=%fused_computation.87 | loop fusion | bytes 8388608 | tf_op jit(solution)/shard_map/slice | solution.py:74
  103.3 4.5 %copy.74 = bf16[2048,8,64]{0,2,1:T(8,128)(2,1)S(1)} copy(bf16[2048,8,64]{2,1,0:T(8,128)(2,1)} %get-tuple-element.198) | data formatting | bytes 4194304 | tf_op jit(solution)/shard_map/slice | solution.py:74
  107.8 1.5 collective-permute-start
  109.4 0.7 collective-permute-done
  110.2 1.1 maximum_convert_fusion
  111.3 5.2 %multiply_convert_fusion = bf16[2048,640]{0,1:T(8,128)(2,1)S(1)} fusion(f32[2051,640]{0,1:T(8,128)S(1)} %maximum_convert_fusion, f32[640]{0:T(1024)S(1)} %get-tuple-element.169, f32[640]{0:T(1024)S(1)} %get-tuple-element.170, f32[640]{0:T(1024)S(1)} %get-tuple-element.171, f32[640]{0:T(1024)S(1)} %get-tuple-element.168, f32[640]{0:T(1024)S(1)} %pad_maximum_fusion.1), kind=kLoop, calls=%fused_computation.29 | loop fusion | flops 17039360 | bytes 23605760 | tf_op jit(solution)/shard_map/convert_element_type | solution.py:41
  117.1 2.0 copy.102
  119.6 2.5 broadcast_multiply_fusion
  122.1 3.0 fusion.24
  125.2 6.8 %while.27 = (s32[]{:T(128)}, f32[8,64,64]{2,1,0:T(8,128)S(1)}, f32[8,8,64,64]{3,2,1,0:T(8,128)}, f32[8,8]{1,0:T(8,128)S(1)}, f32[8,8,64,64]{3,2,1,0:T(8,128)S(1)}, /*index=5*/s32[]{:T(128)}, s32[]{:T(128)}) while((s32[]{:T(128)}, f32[8,64,64]{2,1,0:T(8,128)S(1)}, f32[8,8,64,64]{3,2,1,0:T(8,128)}, f32[8,8]{1,0:T(8,128)S(1)}, ...), condition=%wide.region_3.4_spmd.clone, body=%wide.region_2.3_spmd.clone.sunk | while | flops 131075 | bytes 786636 | solution.py:111
  127.7 0.7 bitcast_dynamic-update-slice_fusion.2
  134.3 70.5 %all-reduce = f32[256]{0:T(256)S(1)} all-reduce(f32[256]{0:T(256)S(1)} %dynamic-update-slice), channel_id=2, replica_groups=mesh['seq'=32,'head'=4] {'seq'}, use_global_device_ids=true, to_apply=%add | all-reduce | flops 256 | bytes 2048
  205.0 4.5 %copy.97 = bf16[2048,8,64]{0,2,1:T(8,128)(2,1)S(1)} copy(bf16[2048,8,64]{2,1,0:T(8,128)(2,1)} %get-tuple-element.199) | data formatting | bytes 4194304
  210.0 22.5 %fusion.2 = f32[8,8,64,256]{3,2,1,0:T(8,128)} fusion(f32[8,8,256]{2,1,0:T(8,128)S(1)} %add_bitcast_fusion.1, f32[8,256,256]{2,1,0:T(8,128)S(1)} %fusion.33, pred[256,256]{1,0:T(8,128)(4,1)S(1)} %iota_compare_fusion, f32[8,256,8,64]{1,0,3,2:T(8,128)} %get-tuple-element.195), kind=kOutput, calls=%fused_computation.7 | convolution fusion | flops 3238002688 | bytes 10616832 | tf_op jit(solution)/shard_map/khts,kshp->kthp/dot_general | solution.py:99
  232.5 35.1 %while.28 = (s32[]{:T(128)}, f32[8,64,64]{2,1,0:T(8,128)S(1)}, s32[]{:T(128)}, f32[32,8]{1,0:T(8,128)S(1)}, f32[32,8,64,64]{3,2,1,0:T(8,128)}, /*index=5*/s32[]{:T(128)}, s32[]{:T(128)}) while((s32[]{:T(128)}, f32[8,64,64]{2,1,0:T(8,128)S(1)}, s32[]{:T(128)}, f32[32,8]{1,0:T(8,128)S(1)}, f32[32,8,64,64]{3,2,1,0:T(8,128)}, ...), condition=%wide.region_7.8_spmd.clone, body=%wide.region_6.7_spmd.clone.sunk | while | flops 131076 | bytes 393425 | solution.py:34
  232.5 1.1 fusion.55
  233.6 1.1 fusion.55
  234.7 1.1 fusion.55
  235.8 1.1 fusion.55
  236.9 1.1 fusion.55
  238.0 1.1 fusion.55
  239.1 1.1 fusion.55
  240.2 1.1 fusion.55
  241.3 1.1 fusion.55
  242.4 1.1 fusion.55
  243.5 1.1 fusion.55
  244.6 1.1 fusion.55
  245.7 1.1 fusion.55
  246.8 1.1 fusion.55
  247.9 1.1 fusion.55
  249.0 1.1 fusion.55
  250.1 1.1 fusion.55
  251.2 1.1 fusion.55
  252.3 1.1 fusion.55
  253.4 1.1 fusion.55
  254.5 1.1 fusion.55
  255.6 1.1 fusion.55
  256.7 1.1 fusion.55
  257.8 1.1 fusion.55
  258.9 1.1 fusion.55
  260.0 1.1 fusion.55
  261.1 1.1 fusion.55
  262.2 1.1 fusion.55
  263.3 1.1 fusion.55
  264.4 1.1 fusion.55
  265.5 1.1 fusion.55
  266.6 1.1 fusion.55
  267.6 4.9 %fusion.23 = f32[8,8,8,8,256]{4,3,2,1,0:T(8,128)S(1)} fusion(f32[8,8,64,256]{3,2,1,0:T(8,128)} %fusion.2, f32[8,8,64,64]{3,2,1,0:T(8,128)} %get-tuple-element.127, f32[8,256,8]{1,2,0:T(8,128)S(1)} %get-tuple-element.192, f32[8,64,64]{2,1,0:T(8,128)S(1)} %get-tuple-element.129, f32[8,8]{1,0:T(8,128)S(1)} %get-tuple-element.202, ...), kind=kOutput, calls=%fused_computation.39 | convolution fusion | flops 807927808 | bytes 9896192 | tf_op jit(solution)/shard_map/ktn,khpn->kthp/dot_general | solution.py:124
  273.2 1.5 copy-done.3
  274.7 2.9 fusion.27
  277.6 3.3 %all_to_all.35 = bf16[4,512,512]{1,0,2:T(4,128)(2,1)S(1)} reshape(bf16[2048,8,64]{0,2,1:T(8,128)(2,1)} %fusion.27) | data formatting | bytes 4194304 | tf_op jit(solution)/shard_map/all_to_all | solution.py:135
  281.4 27.9 %all_to_all.40 = bf16[4,512,512]{1,2,0:T(8,128)(2,1)S(1)} all-to-all(bf16[4,512,512]{1,2,0:T(8,128)(2,1)S(1)} %copy.88), channel_id=1, replica_groups=mesh['seq'=32,'head'=4] {'head'}, dimensions={0} | all-to-all | bytes 4194304 | tf_op jit(solution)/shard_map/all_to_all | solution.py:135
  310.3 1.1 copy-done.12
  311.4 3.4 %convolution_convert_fusion.1 = bf16[512,1024]{1,0:T(8,128)(2,1)} fusion(bf16[512,2048]{0,1:T(8,128)(2,1)S(1)} %fusion.22, bf16[2048,1024]{1,0:T(8,128)(2,1)S(1)} %copy-done.12), kind=kOutput, calls=%fused_computation.52 | convolution fusion | flops 2148007936 | bytes 7340032 | tf_op jit(solution)/shard_map/dot_general | solution.py:139
  (132 shorter events, 14.1 us)
Async XLA Ops:
  6.5 1.2 copy-start
  11.3 15.6 %all-to-all-start.1 = ((bf16[4,2,2048]{2,1,0:T(2,128)(2,1)}), bf16[4,2,2048]{2,1,0:T(2,128)(2,1)S(1)}, u32[]{:S(2)}, u32[]{:S(2)}) async-start(bf16[4,2,2048]{2,1,0:T(2,128)(2,1)} %reshape.184), calls=%async_computation.1 | async-start | bytes 65536 | tf_op jit(solution)/shard_map/all_to_all | solution.py:68
  26.9 5.1 %copy-start.6 = (f32[4,512]{1,0:T(4,128)S(1)}, f32[4,512]{1,0:T(4,128)}, u32[]{:S(2)}) copy-start(f32[4,512]{1,0:T(4,128)} %param.19) | copy-start | bytes 24580
  26.9 5.2 %copy-start.7 = (f32[4,128]{1,0:T(4,128)S(1)}, f32[4,128]{1,0:T(4,128)}, u32[]{:S(2)}) copy-start(f32[4,128]{1,0:T(4,128)} %param.21) | copy-start | bytes 6148
  26.9 5.2 %copy-start.8 = (f32[512]{0:T(512)S(1)}, f32[512]{0:T(512)}, u32[]{:S(2)}) copy-start(f32[512]{0:T(512)} %param.20) | copy-start | bytes 6148
  26.9 5.2 %copy-start.11 = (f32[128]{0:T(128)S(1)}, f32[128]{0:T(128)}, u32[]{:S(2)}) copy-start(f32[128]{0:T(128)} %param.22) | copy-start | bytes 1540
  26.9 61.9 %copy-start.13 = (f32[8]{0:T(128)S(1)}, f32[8]{0:T(128)}, u32[]{:S(2)}) copy-start(f32[8]{0:T(128)} %param.24) | copy-start | bytes 100
  27.0 62.0 %copy-start.9 = (f32[8]{0:T(128)S(1)}, f32[8]{0:T(128)}, u32[]{:S(2)}) copy-start(f32[8]{0:T(128)} %param.23) | copy-start | bytes 100
  27.0 67.4 %all-to-all-start = ((bf16[512,32,128]{2,0,1:T(8,128)(2,1)}), bf16[512,32,128]{2,0,1:T(8,128)(2,1)}, u32[]{:S(2)}, u32[]{:S(2)}) async-start(bf16[512,32,128]{2,0,1:T(8,128)(2,1)} %bitcast.113), calls=%async_computation | async-start | bytes 8388608 | tf_op jit(solution)/shard_map/all_to_all | solution.py:67
  32.0 200.5 %all-gather.4.cloned.1.call-start = ((), (), s32[]{:S(2)}) async-start(), calls=%async_computation.3 | async-start | bytes 8650752 | tf_op jit(solution)/shard_map/all_gather | solution.py:22
  107.8 2.3 collective-permute-start
  117.1 2.5 copy-start.2
  125.2 7.6 %copy-start.14 = (u32[128]{0:T(128)S(1)}, u32[128]{0:T(128)}, u32[]{:S(2)}) copy-start(u32[128]{0:T(128)} %constant.66) | copy-start | bytes 1540
  132.0 0.7 copy-start.4
  272.5 2.2 copy-start.3
  272.5 2.2 copy-start.10
  281.3 28.4 %copy-start.5 = (f32[2048]{0:T(1024)S(1)}, f32[2048]{0:T(1024)}, u32[]{:S(2)}) copy-start(f32[2048]{0:T(1024)} %param.26) | copy-start | bytes 24580
  309.2 2.2 copy-start.12
  309.7 5.0 %copy-start.1 = (bf16[512,1024]{1,0:T(8,128)(2,1)S(1)}, bf16[512,1024]{1,0:T(8,128)(2,1)}, u32[]{:S(2)}) copy-start(bf16[512,1024]{1,0:T(8,128)(2,1)} %param.16) | copy-start | bytes 3145732
Sparse Core Ops, SparseCore 0:
  132.8 58.4 all-gather.3
where the time goes:
time: 323 us; the launch traced here: 322 us
  blocking collectives  155 us (48%)
  other arithmetic  59.8 us (19%)
  matrix products  43.9 us (14%)
  local copies, waits for them, and re-layouts  35.4 us (11%)
  between operations  14.5 us (4%)
  starting transfers between devices  10.9 us (3%)
    unnamed x1, blocking collectives  70.5 us
    all_gather x1, blocking collectives, on_device(): bc_rows = lax.all_gather(bc_dt[:, :2 * STATE], 'head', axis=0, tiled=True)  56.7 us
    select_n x32, other arithmetic, hop(): return jax.tree.map(lambda a, b: jnp.where(reached, a, b), new, before)  33.7 us
    all_to_all x1, blocking collectives, on_device(): lax.all_to_all(gated_out, 'head', split_axis=0, concat_axis=1, tiled=True)  27.9 us
    dot_general x1, matrix products, on_device(): jnp.einsum('khts,kshp->kthp', mixed, xdt_blocks, precision=highest)  22.5 us
    unnamed x42, local copies, waits for them, and re-layouts  13.7 us
    slice x2, local copies, waits for them, and re-layouts, on_device(): x_chan = gate_x[:, :, HEAD_DIM:].reshape(seq_rows, dinner_here)  8.44 us
    dot_general x1, matrix products, on_device(): jnp.dot(tokens, w_gate_x, preferred_element_type=jnp.float32)  8.12 us
  transfers between devices with their start and end apart: 4, of which 1 were waited for; matrix products, arithmetic and copies ran while one was open for 14% of the time, Pallas kernels for 0%

commit v1 on v0

--- a/solution.py
+++ b/solution.py
@@ -68,7 +68,23 @@
         lax.all_to_all(dt_all, "head", split_axis=1, concat_axis=0, tiled=True),
     )
     dt_raw = dt_raw[:, :, 0]
-    bc_rows = lax.all_gather(bc_dt[:, : 2 * STATE], "head", axis=0, tiled=True)
+    x = bc_dt[:, : 2 * STATE]
+    size_2, here, rows = (lax.axis_size("head"), lax.axis_index("head"), x.shape[0])
+    ahead = [(i_2, (i_2 + 1) % size_2) for i_2 in range(size_2)]
+    left = [(i_2, (i_2 - 1) % size_2) for i_2 in range(size_2)]
+    out = jnp.zeros((*x.shape[:0], size_2 * rows, *x.shape[0 + 1 :]), x.dtype)
+    out = lax.dynamic_update_slice_in_dim(out, x, here * rows, axis=0)
+    from_left = from_right = x
+    half = size_2 // 2
+    for step in range(1, half + 1):
+        from_left = lax.ppermute(from_left, "head", ahead)
+        out = lax.dynamic_update_slice_in_dim(out, from_left, (here - step) % size_2 * rows, axis=0)
+        if step < size_2 - half:
+            from_right = lax.ppermute(from_right, "head", left)
+            out = lax.dynamic_update_slice_in_dim(
+                out, from_right, (here + step) % size_2 * rows, axis=0
+            )
+    bc_rows = out
     seq_rows = gate_x.shape[0]
     gate_z = gate_x[:, :, :HEAD_DIM]
     x_chan = gate_x[:, :, HEAD_DIM:].reshape(seq_rows, dinner_here)

time: 323 us -> 319 us (0.988)
  blocking collectives: 155 us -> 98.4 us
  waiting for transfers between devices: 0.77 us -> 49.1 us
  starting transfers between devices: 10.9 us -> 14.3 us
    all_gather x1 -> x0, blocking collectives: 56.7 us -> none  [on_device(): bc_rows = lax.all_gather(bc_dt[:, :2 * STATE], 'head', axis=0, tiled=True)]
    ppermute x0 -> x3, waiting for transfers between devices: none -> 48.3 us  [the longest x2 48.3 us: on_device(): from_left = lax.ppermute(from_left, 'head', ahead)]
    ppermute x0 -> x3, starting transfers between devices: none -> 3.38 us  [the longest x2 2.13 us: on_device(): from_left = lax.ppermute(from_left, 'head', ahead)]
  transfers between devices with their start and end apart: 4 -> 7, of which waited for: 1 -> 3; matrix products, arithmetic and copies ran while one was open for 14% -> 14% of each run, Pallas kernels for 0% -> 0%
where the time goes in v1:
time: 319 us; the launch traced here: 317 us
  blocking collectives  98.4 us (31%)
  other arithmetic  59.8 us (19%)
  waiting for transfers between devices  49.1 us (15%)
  matrix products  43.9 us (14%)
  local copies, waits for them, and re-layouts  35.6 us (11%)
  between operations  14.6 us (5%)
  starting transfers between devices  14.3 us (4%)
    unnamed x1, blocking collectives  70.5 us
    ppermute x2, waiting for transfers between devices, on_device(): from_left = lax.ppermute(from_left, 'head', ahead)  48.3 us
    select_n x32, other arithmetic, hop(): return jax.tree.map(lambda a, b: jnp.where(reached, a, b), new, before)  33.7 us
    all_to_all x1, blocking collectives, on_device(): lax.all_to_all(gated_out, 'head', split_axis=0, concat_axis=1, tiled=True)  28 us
    dot_general x1, matrix products, on_device(): jnp.einsum('khts,kshp->kthp', mixed, xdt_blocks, precision=highest)  22.5 us
    unnamed x42, local copies, waits for them, and re-layouts  13.7 us
    slice x2, local copies, waits for them, and re-layouts, on_device(): x_chan = gate_x[:, :, HEAD_DIM:].reshape(seq_rows, dinner_here)  8.43 us
    dot_general x1, matrix products, on_device(): jnp.dot(tokens, w_gate_x, preferred_element_type=jnp.float32)  8.12 us
  transfers between devices with their start and end apart: 7, of which 3 were waited for; matrix products, arithmetic and copies ran while one was open for 14% of the time, Pallas kernels for 0%

profile of v1, /device:TPU:0, one launch (start us, length us, event | category | flops | bytes accessed | tf_op | source)
XLA Modules:
  0.0 316.8 jit_solution(14234853545892994531)
XLA Ops:
  6.5 1.2 copy-done
  7.8 1.5 convolution_convert_fusion.2
  11.3 4.4 %all-to-all-start.1 = ((bf16[4,2,2048]{2,1,0:T(2,128)(2,1)}), bf16[4,2,2048]{2,1,0:T(2,128)(2,1)S(1)}, u32[]{:S(2)}, u32[]{:S(2)}) async-start(bf16[4,2,2048]{2,1,0:T(2,128)(2,1)} %reshape.184), calls=%async_computation.1 | async-start | bytes 65536 | tf_op jit(solution)/shard_map/all_to_all | solution.py:68
  15.7 8.1 %fusion.28 = bf16[64,32,8,128]{3,2,1,0:T(8,128)(2,1)S(1)} fusion(bf16[512,1024]{1,0:T(8,128)(2,1)S(1)} %copy-done, bf16[1024,4096]{1,0:T(8,128)(2,1)} %param.17), kind=kOutput, calls=%fused_computation.46 | convolution fusion | flops 4297064448 | bytes 13631488 | tf_op jit(solution)/shard_map/dot_general | solution.py:62
  23.8 3.1 copy.126
  27.0 5.0 %all-to-all-start = ((bf16[512,32,128]{2,0,1:T(8,128)(2,1)}), bf16[512,32,128]{2,0,1:T(8,128)(2,1)}, u32[]{:S(2)}, u32[]{:S(2)}) async-start(bf16[512,32,128]{2,0,1:T(8,128)(2,1)} %bitcast.113), calls=%async_computation | async-start | bytes 8388608 | tf_op jit(solution)/shard_map/all_to_all | solution.py:67
  32.1 2.1 collective-permute-start
  34.2 1.2 collective-permute-start.1
  35.8 4.5 %reduce-window.6 = f32[8,8,2,128]{3,1,2,0:T(8,128)S(1)} reduce-window(f32[8,8,2,128]{3,1,2,0:T(8,128)S(1)} %get-tuple-element.196, f32[]{:T(128)} %constant.95.clone.1), window={size=1x1x1x128 pad=0_0x0_0x0_0x127_0}, to_apply=%region_0.1 | reduce-window | flops 2080768 | bytes 131076 | tf_op jit(solution)/shard_map/reduce-window
  41.1 42.2 %collective-permute-done = bf16[512,128]{0,1:T(8,128)(2,1)S(1)} collective-permute-done((bf16[512,128]{0,1:T(8,128)(2,1)S(1)}, bf16[512,128]{0,1:T(8,128)(2,1)S(1)}, u32[]{:S(2)}, u32[]{:S(2)}) %collective-permute-start) | collective-permute-done | bytes 131104 | tf_op jit(solution)/shard_map/ppermute | solution.py:80
  83.3 6.1 %collective-permute-done.2 = bf16[512,128]{0,1:T(8,128)(2,1)S(1)} collective-permute-done((bf16[512,128]{0,1:T(8,128)(2,1)S(1)}, bf16[512,128]{0,1:T(8,128)(2,1)S(1)}, u32[]{:S(2)}, u32[]{:S(2)}) %collective-permute-start.2) | collective-permute-done | bytes 131104 | tf_op jit(solution)/shard_map/ppermute | solution.py:80
  89.4 4.9 %copy.76 = bf16[4,512,8,128]{3,2,1,0:T(8,128)(2,1)S(1)} copy(bf16[4,512,8,128]{3,1,2,0:T(8,128)(2,1)} %bitcast.2) | data formatting | bytes 8388608 | tf_op jit(solution)/shard_map/all_to_all | solution.py:67
  94.3 4.0 %fusion.44 = (bf16[2048,8,64]{2,1,0:T(8,128)(2,1)}, bf16[2048,8,64]{2,1,0:T(8,128)(2,1)}) fusion(bf16[2048,8,128]{2,1,0:T(8,128)(2,1)S(1)} %bitcast.109), kind=kLoop, calls=%fused_computation.91 | loop fusion | bytes 8388608 | tf_op jit(solution)/shard_map/slice | solution.py:90
  98.3 4.5 %copy.77 = bf16[2048,8,64]{0,2,1:T(8,128)(2,1)S(1)} copy(bf16[2048,8,64]{2,1,0:T(8,128)(2,1)} %get-tuple-element.198) | data formatting | bytes 4194304 | tf_op jit(solution)/shard_map/slice | solution.py:90
  102.9 1.5 collective-permute-start.3
  105.2 1.1 maximum_convert_fusion
  106.4 5.2 %multiply_convert_fusion = bf16[2048,640]{0,1:T(8,128)(2,1)S(1)} fusion(f32[2051,640]{0,1:T(8,128)S(1)} %maximum_convert_fusion, f32[640]{0:T(1024)S(1)} %get-tuple-element.169, f32[640]{0:T(1024)S(1)} %get-tuple-element.170, f32[640]{0:T(1024)S(1)} %get-tuple-element.171, f32[640]{0:T(1024)S(1)} %get-tuple-element.168, f32[640]{0:T(1024)S(1)} %pad_maximum_fusion.1), kind=kLoop, calls=%fused_computation.29 | loop fusion | flops 17039360 | bytes 23605760 | tf_op jit(solution)/shard_map/convert_element_type | solution.py:41
  112.2 2.0 copy.105
  114.7 2.5 broadcast_multiply_fusion
  117.2 3.0 fusion.24
  120.2 6.8 %while.27 = (s32[]{:T(128)}, f32[8,64,64]{2,1,0:T(8,128)S(1)}, f32[8,8,64,64]{3,2,1,0:T(8,128)}, f32[8,8]{1,0:T(8,128)S(1)}, f32[8,8,64,64]{3,2,1,0:T(8,128)S(1)}, /*index=5*/s32[]{:T(128)}, s32[]{:T(128)}) while((s32[]{:T(128)}, f32[8,64,64]{2,1,0:T(8,128)S(1)}, f32[8,8,64,64]{3,2,1,0:T(8,128)}, f32[8,8]{1,0:T(8,128)S(1)}, ...), condition=%wide.region_3.4_spmd.clone, body=%wide.region_2.3_spmd.clone.sunk | while | flops 131075 | bytes 786636 | solution.py:127
  129.4 70.5 %all-reduce = f32[256]{0:T(256)S(1)} all-reduce(f32[256]{0:T(256)S(1)} %dynamic-update-slice), channel_id=2, replica_groups=mesh['seq'=32,'head'=4] {'seq'}, use_global_device_ids=true, to_apply=%add | all-reduce | flops 256 | bytes 2048
  200.0 4.5 %copy.100 = bf16[2048,8,64]{0,2,1:T(8,128)(2,1)S(1)} copy(bf16[2048,8,64]{2,1,0:T(8,128)(2,1)} %get-tuple-element.199) | data formatting | bytes 4194304
  205.1 22.5 %fusion.2 = f32[8,8,64,256]{3,2,1,0:T(8,128)} fusion(f32[8,8,256]{2,1,0:T(8,128)S(1)} %add_bitcast_fusion.1, f32[8,256,256]{2,1,0:T(8,128)S(1)} %fusion.33, pred[256,256]{1,0:T(8,128)(4,1)S(1)} %iota_compare_fusion, f32[8,256,8,64]{1,0,3,2:T(8,128)} %get-tuple-element.195), kind=kOutput, calls=%fused_computation.7 | convolution fusion | flops 3238002688 | bytes 10616832 | tf_op jit(solution)/shard_map/khts,kshp->kthp/dot_general | solution.py:115
  227.6 35.1 %while.28 = (s32[]{:T(128)}, f32[8,64,64]{2,1,0:T(8,128)S(1)}, s32[]{:T(128)}, f32[32,8]{1,0:T(8,128)S(1)}, f32[32,8,64,64]{3,2,1,0:T(8,128)}, /*index=5*/s32[]{:T(128)}, s32[]{:T(128)}) while((s32[]{:T(128)}, f32[8,64,64]{2,1,0:T(8,128)S(1)}, s32[]{:T(128)}, f32[32,8]{1,0:T(8,128)S(1)}, f32[32,8,64,64]{3,2,1,0:T(8,128)}, ...), condition=%wide.region_7.8_spmd.clone, body=%wide.region_6.7_spmd.clone.sunk | while | flops 131076 | bytes 393425 | solution.py:34
  227.6 1.1 fusion.56
  228.7 1.1 fusion.56
  229.8 1.1 fusion.56
  230.9 1.1 fusion.56
  232.0 1.1 fusion.56
  233.1 1.1 fusion.56
  234.2 1.1 fusion.56
  235.3 1.1 fusion.56
  236.4 1.1 fusion.56
  237.5 1.1 fusion.56
  238.6 1.1 fusion.56
  239.7 1.1 fusion.56
  240.8 1.1 fusion.56
  241.9 1.1 fusion.56
  243.0 1.1 fusion.56
  244.1 1.1 fusion.56
  245.2 1.1 fusion.56
  246.3 1.1 fusion.56
  247.4 1.1 fusion.56
  248.5 1.1 fusion.56
  249.6 1.1 fusion.56
  250.7 1.1 fusion.56
  251.8 1.1 fusion.56
  252.9 1.1 fusion.56
  254.0 1.1 fusion.56
  255.1 1.1 fusion.56
  256.2 1.1 fusion.56
  257.3 1.1 fusion.56
  258.4 1.1 fusion.56
  259.5 1.1 fusion.56
  260.6 1.1 fusion.56
  261.7 1.1 fusion.56
  262.7 4.9 %fusion.23 = f32[8,8,8,8,256]{4,3,2,1,0:T(8,128)S(1)} fusion(f32[8,8,64,256]{3,2,1,0:T(8,128)} %fusion.2, f32[8,8,64,64]{3,2,1,0:T(8,128)} %get-tuple-element.127, f32[8,256,8]{1,2,0:T(8,128)S(1)} %get-tuple-element.192, f32[8,64,64]{2,1,0:T(8,128)S(1)} %get-tuple-element.129, f32[8,8]{1,0:T(8,128)S(1)} %get-tuple-element.204, ...), kind=kOutput, calls=%fused_computation.39 | convolution fusion | flops 807927808 | bytes 9896192 | tf_op jit(solution)/shard_map/ktn,khpn->kthp/dot_general | solution.py:140
  268.3 1.5 copy-done.3
  269.8 2.9 fusion.27
  272.7 3.3 %all_to_all.35 = bf16[4,512,512]{1,0,2:T(4,128)(2,1)S(1)} reshape(bf16[2048,8,64]{0,2,1:T(8,128)(2,1)} %fusion.27) | data formatting | bytes 4194304 | tf_op jit(solution)/shard_map/all_to_all | solution.py:151
  276.4 28.0 %all_to_all.40 = bf16[4,512,512]{1,2,0:T(8,128)(2,1)S(1)} all-to-all(bf16[4,512,512]{1,2,0:T(8,128)(2,1)S(1)} %copy.91), channel_id=1, replica_groups=mesh['seq'=32,'head'=4] {'head'}, dimensions={0} | all-to-all | bytes 4194304 | tf_op jit(solution)/shard_map/all_to_all | solution.py:151
  305.5 1.1 copy-done.12
  306.6 3.4 %convolution_convert_fusion.1 = bf16[512,1024]{1,0:T(8,128)(2,1)} fusion(bf16[512,2048]{0,1:T(8,128)(2,1)S(1)} %fusion.22, bf16[2048,1024]{1,0:T(8,128)(2,1)S(1)} %copy-done.12), kind=kOutput, calls=%fused_computation.52 | convolution fusion | flops 2148007936 | bytes 7340032 | tf_op jit(solution)/shard_map/dot_general | solution.py:155
  (141 shorter events, 16.6 us)
Async XLA Ops:
  6.5 1.2 copy-start
  11.3 15.6 %all-to-all-start.1 = ((bf16[4,2,2048]{2,1,0:T(2,128)(2,1)}), bf16[4,2,2048]{2,1,0:T(2,128)(2,1)S(1)}, u32[]{:S(2)}, u32[]{:S(2)}) async-start(bf16[4,2,2048]{2,1,0:T(2,128)(2,1)} %reshape.184), calls=%async_computation.1 | async-start | bytes 65536 | tf_op jit(solution)/shard_map/all_to_all | solution.py:68
  26.9 8.6 %copy-start.6 = (f32[4,512]{1,0:T(4,128)S(1)}, f32[4,512]{1,0:T(4,128)}, u32[]{:S(2)}) copy-start(f32[4,512]{1,0:T(4,128)} %param.19) | copy-start | bytes 24580
  26.9 8.6 %copy-start.7 = (f32[4,128]{1,0:T(4,128)S(1)}, f32[4,128]{1,0:T(4,128)}, u32[]{:S(2)}) copy-start(f32[4,128]{1,0:T(4,128)} %param.21) | copy-start | bytes 6148
  26.9 8.6 %copy-start.8 = (f32[512]{0:T(512)S(1)}, f32[512]{0:T(512)}, u32[]{:S(2)}) copy-start(f32[512]{0:T(512)} %param.20) | copy-start | bytes 6148
  26.9 8.6 %copy-start.11 = (f32[128]{0:T(128)S(1)}, f32[128]{0:T(128)}, u32[]{:S(2)}) copy-start(f32[128]{0:T(128)} %param.22) | copy-start | bytes 1540
  26.9 8.6 %copy-start.13 = (f32[8]{0:T(128)S(1)}, f32[8]{0:T(128)}, u32[]{:S(2)}) copy-start(f32[8]{0:T(128)} %param.24) | copy-start | bytes 100
  27.0 8.7 %copy-start.9 = (f32[8]{0:T(128)S(1)}, f32[8]{0:T(128)}, u32[]{:S(2)}) copy-start(f32[8]{0:T(128)} %param.23) | copy-start | bytes 100
  27.0 62.5 %all-to-all-start = ((bf16[512,32,128]{2,0,1:T(8,128)(2,1)}), bf16[512,32,128]{2,0,1:T(8,128)(2,1)}, u32[]{:S(2)}, u32[]{:S(2)}) async-start(bf16[512,32,128]{2,0,1:T(8,128)(2,1)} %bitcast.113), calls=%async_computation | async-start | bytes 8388608 | tf_op jit(solution)/shard_map/all_to_all | solution.py:67
  32.0 195.6 %all-gather.4.cloned.1.call-start = ((), (), s32[]{:S(2)}) async-start(), calls=%async_computation.3 | async-start | bytes 8650752 | tf_op jit(solution)/shard_map/all_gather | solution.py:22
  32.1 51.1 %collective-permute-start = (bf16[512,128]{0,1:T(8,128)(2,1)S(1)}, bf16[512,128]{0,1:T(8,128)(2,1)S(1)}, u32[]{:S(2)}, u32[]{:S(2)}) collective-permute-start(bf16[512,128]{0,1:T(8,128)(2,1)S(1)} %get-tuple-element.202), channel_id=1, source_target_pairs={{0,1},{1,2},{2,3},{3,0},{4,5},{5,6},{6,7},{7,4},{8,9},{9,10},{10,1... | collective-permute-start | bytes 393224 | tf_op jit(solution)/shard_map/ppermute | solution.py:80
  34.2 49.0 %collective-permute-start.1 = (bf16[512,128]{0,1:T(8,128)(2,1)S(1)}, bf16[512,128]{0,1:T(8,128)(2,1)S(1)}, u32[]{:S(2)}, u32[]{:S(2)}) collective-permute-start(bf16[512,128]{0,1:T(8,128)(2,1)S(1)} %get-tuple-element.202), channel_id=1, source_target_pairs={{0,3},{1,0},{2,1},{3,2},{4,7},{5,4},{6,5},{7,6},{8,11},{9,8},{10,9... | collective-permute-start | bytes 393224 | tf_op jit(solution)/shard_map/ppermute | solution.py:83
  83.2 6.2 %collective-permute-start.2 = (bf16[512,128]{0,1:T(8,128)(2,1)S(1)}, bf16[512,128]{0,1:T(8,128)(2,1)S(1)}, u32[]{:S(2)}, u32[]{:S(2)}) collective-permute-start(bf16[512,128]{0,1:T(8,128)(2,1)S(1)} %collective-permute-done), channel_id=1, source_target_pairs={{0,1},{1,2},{2,3},{3,0},{4,5},{5,6},{6,7},{7,4},{8,9},{9,10},{10,1... | collective-permute-start | bytes 393224 | tf_op jit(solution)/shard_map/ppermute | solution.py:80
  102.9 2.3 collective-permute-start.3
  112.2 2.5 copy-start.2
  120.2 7.6 %copy-start.14 = (u32[128]{0:T(128)S(1)}, u32[128]{0:T(128)}, u32[]{:S(2)}) copy-start(u32[128]{0:T(128)} %constant.102) | copy-start | bytes 1540
  127.0 0.7 copy-start.4
  267.6 2.2 copy-start.3
  267.6 2.2 copy-start.10
  276.4 28.5 %copy-start.5 = (f32[2048]{0:T(1024)S(1)}, f32[2048]{0:T(1024)}, u32[]{:S(2)}) copy-start(f32[2048]{0:T(1024)} %param.26) | copy-start | bytes 24580
  304.4 2.2 copy-start.12
  305.0 5.0 %copy-start.1 = (bf16[512,1024]{1,0:T(8,128)(2,1)S(1)}, bf16[512,1024]{1,0:T(8,128)(2,1)}, u32[]{:S(2)}) copy-start(bf16[512,1024]{1,0:T(8,128)(2,1)} %param.16) | copy-start | bytes 3145732
Sparse Core Ops, SparseCore 0:
  127.9 57.4 all-gather.3
